TPU v7x, 256 devices: a whole 4x4x8 slice. The times are simulated.
256 devices in a mesh: row: 8 (over x, core), col: 32 (over y, z).
Axes of the slice: x: 4, y: 4, z: 8, core: 2. Of those that a mesh axis runs over, the one named last changes fastest.
Arguments:
- deflation: bfloat16 [16, 256, 16, 3072], P('row', 'col'), may hold values from 0 to 0.019897461
- coefficient: float32 [16, 256, 16], P('row', 'col'), may hold values from 1 to 10
- gradients: bfloat16 [3, 64, 64], replicated, may hold values from -0.75 to 0.75
- x_penalty: float32 [24, 256, 16], P('row', 'col'), may hold values from 1 to 10, as said below
- y_penalty: float32 [16, 288, 16], P('row', 'col'), may hold values from 1 to 10, as said below
- z_penalty: float32 [16, 256, 17], P('row', 'col'), may hold values from 1 to 10
- coarse_order: int32 [1024], replicated, may hold values from 0 to 1023, as said below
Outputs:
- coarse_blocks: float32 [1024, 7, 2304], P(('row', 'col'))
- panel: float32 [1024, 48, 528], P(('row', 'col'))
Inputs may be any that keep to these rules, and one draw needn't show every extreme that they name: `coarse_order`: each subdomain number appears once; subdomains with consecutive coarse numbers are mostly neighbours along the third or second dimension. `x_penalty`: row i * 3 + 2 equals row (i + 1) * 3: a face between two devices' blocks is held by both. `y_penalty`: column j * 9 + 8 equals column (j + 1) * 9: a face between two devices' blocks is held by both.
All inputs are finite; a program needn't handle non-finite values.
Results may differ from a plain program's by a relative error of at most 0.00044.
Values may be sent and summed in bfloat16 or wider, within the bound.
No kernel may reach another device: no remote copies, remote signals or barrier semaphores. Data moves between devices by JAX's collectives and lax.ppermute only.
A program may use at most 128 MiB of HBM per device.

v0:
```python
import jax
import jax.numpy as jnp
from jax import lax
from jax.sharding import PartitionSpec as P

NV = 48
SUB_DEV = 4
PB = 11
LINE_WEIGHTS = (1.0 / 6.0, 5.0 / 6.0, 5.0 / 6.0, 1.0 / 6.0)


def with_halo(shard, sides, width):
    for axis, dim in sides:
        size, length = (lax.axis_size(axis), shard.shape[dim])
        up = [(i, (i + 1) % size) for i in range(size - 1)]
        down = [(j, i) for i, j in up]
        last = lax.slice_in_dim(shard, length - width, length, axis=dim)
        initial = lax.slice_in_dim(shard, 0, width, axis=dim)
        before = lax.ppermute(last, axis, up)
        after = lax.ppermute(initial, axis, down)
        shard = jnp.concatenate([before, shard, after], axis=dim)
    return shard


def node_weights():
    line = jnp.array(LINE_WEIGHTS, jnp.float32)
    return (line[:, None, None] * line[None, :, None] * line[None, None, :]).reshape(64)


def contract(form, left, right):
    return jnp.einsum(form, left, right, preferred_element_type=jnp.float32)


def traces(values, axis, side):
    lead = values.ndim - 1
    nodes = values.reshape(values.shape[:lead] + (4, 4, 4, NV))
    picked = lax.index_in_dim(nodes, side, lead + axis, keepdims=False)
    return picked.reshape(values.shape[:lead] + (16, NV))


def scaled(trace, root):
    return (root[..., None, None] * trace.astype(jnp.float32)).astype(jnp.bfloat16)


def grouped(left, right, groups):
    shape = left.shape
    split = shape[:2] + (groups, shape[2] // groups) + shape[3:]
    return contract("xyskav,xyskaw->svw", left.reshape(split), right.reshape(split))


def lateral(plus, minus, root, below, above, groups):
    jump = (
        root[1:-1, :, :, None, None]
        * (plus[:-1].astype(jnp.float32) - minus[1:].astype(jnp.float32))
    ).astype(jnp.bfloat16)
    low_own = scaled(minus[0], root[0])
    low_other = scaled(below, root[0])
    high_own = scaled(plus[-1], root[-1])
    high_other = scaled(above, root[-1])
    self_part = (
        grouped(jump, jump, groups)
        + grouped(low_own[None], low_own[None], groups)
        + grouped(high_own[None], high_own[None], groups)
    )
    return (
        self_part,
        -grouped(low_own[None], low_other[None], groups),
        -grouped(high_own[None], high_other[None], groups),
    )


def vertical(plus, minus, root, groups):
    width, length, depth = plus.shape[:3]
    height = depth // groups
    plus = plus.reshape(width, length, groups, height, 16, NV)
    minus = minus.reshape(width, length, groups, height, 16, NV)
    inner_root = root[:, :, :depth].reshape(width, length, groups, height)[:, :, :, 1:]
    jump = (
        inner_root[..., None, None]
        * (plus[:, :, :, :-1].astype(jnp.float32) - minus[:, :, :, 1:].astype(jnp.float32))
    ).astype(jnp.bfloat16)
    edge_root = root[:, :, ::height]
    first = minus[:, :, :, 0]
    last = plus[:, :, :, -1]
    blank = jnp.zeros_like(last[:, :, :1])
    low_own = scaled(first, edge_root[:, :, :groups])
    low_other = scaled(jnp.concatenate([blank, last[:, :, :-1]], axis=2), edge_root[:, :, :groups])
    high_own = scaled(last, edge_root[:, :, 1:])
    high_other = scaled(jnp.concatenate([first[:, :, 1:], blank], axis=2), edge_root[:, :, 1:])
    pairing = "xysav,xysaw->svw"
    self_part = (
        contract("xyskav,xyskaw->svw", jump, jump)
        + contract(pairing, low_own, low_own)
        + contract(pairing, high_own, high_own)
    )
    return (
        self_part,
        -contract(pairing, low_own, low_other),
        -contract(pairing, high_own, high_other),
    )


def volume(values, coefficient, gradients, groups):
    width, length, depth = values.shape[:3]
    nodes = values.reshape(width, length, depth, 64, NV)
    factor = jnp.sqrt(coefficient[..., None] * node_weights())
    total = jnp.zeros((groups, NV, NV), jnp.float32)
    for axis in range(3):
        product = contract("ab,xyzbv->xyzav", gradients[axis], nodes)
        rounded = (product * factor[..., None]).astype(jnp.bfloat16)
        rounded = rounded.reshape(width, length, groups, depth // groups, 64, NV)
        total = total + contract("xyskav,xyskaw->svw", rounded, rounded)
    return total


def panel_rows(blocks, column_block, present):
    picks = (
        present[:, :, None]
        & (column_block[:, :, None] == jnp.arange(PB, dtype=jnp.int32)[None, None, :])
    ).astype(jnp.float32)
    rows = jnp.einsum("stp,stvw->svpw", picks, blocks, precision=lax.Precision.HIGHEST).reshape(
        blocks.shape[0], NV, PB * NV
    )
    select = (column_block[:, :1] == jnp.arange(PB, dtype=jnp.int32)[None, :]).astype(jnp.float32)
    share = jnp.einsum("sp,svq->pvq", select, rows, precision=lax.Precision.HIGHEST)
    return (rows, select, share)


def finish(rows, select, assembled):
    whole = assembled.reshape(PB * NV, PB * NV)
    factor = jnp.linalg.cholesky(0.5 * (whole + whole.T))
    count = rows.shape[0]
    solved = jax.scipy.linalg.solve_triangular(
        factor, rows.reshape(count * NV, PB * NV).T, lower=True
    ).T.reshape(count, NV, PB * NV)
    inside = jnp.einsum(
        "sp,pvq->svq", select, factor.reshape(PB, NV, PB * NV), precision=lax.Precision.HIGHEST
    )
    return jnp.where(jnp.sum(select, axis=1)[:, None, None] > 0, inside, solved)


def shards(deflation, coefficient, gradients, x_penalty, y_penalty, z_penalty, coarse_order):
    plus_x = traces(deflation, 0, 3)
    minus_x = traces(deflation, 0, 0)
    plus_y = traces(deflation, 1, 3)
    minus_y = traces(deflation, 1, 0)
    padded = with_halo(deflation, (("row", 0), ("col", 1)), 1)
    below_x = traces(padded[0, 1:-1], 0, 3)
    above_x = traces(padded[-1, 1:-1], 0, 0)
    below_y = traces(padded[1:-1, 0], 1, 3)
    above_y = traces(padded[1:-1, -1], 1, 0)
    x_root = jnp.sqrt(x_penalty)
    y_root = jnp.sqrt(y_penalty)
    z_root = jnp.sqrt(z_penalty)
    self_x, low_x, high_x = lateral(plus_x, minus_x, x_root, below_x, above_x, SUB_DEV)
    self_y, low_y, high_y = lateral(
        jnp.swapaxes(plus_y, 0, 1),
        jnp.swapaxes(minus_y, 0, 1),
        jnp.swapaxes(y_root, 0, 1),
        below_y,
        above_y,
        SUB_DEV,
    )
    self_z, low_z, high_z = vertical(
        traces(deflation, 2, 3), traces(deflation, 2, 0), z_root, SUB_DEV
    )
    diagonal = volume(deflation, coefficient, gradients, SUB_DEV) + self_x + self_y + self_z
    blocks = jnp.stack([diagonal, low_x, high_x, low_y, high_y, low_z, high_z], axis=1)
    row_pos = lax.axis_index("row")
    col_pos = lax.axis_index("col")
    row_count = lax.axis_size("row")
    col_count = lax.axis_size("col")
    device = row_pos * col_count + col_pos
    local = jnp.arange(SUB_DEV, dtype=jnp.int32)
    owner = device * SUB_DEV + local
    stride = col_count * SUB_DEV
    neighbours = jnp.stack(
        [
            owner,
            owner - stride,
            owner + stride,
            owner - SUB_DEV,
            owner + SUB_DEV,
            owner - 1,
            owner + 1,
        ],
        axis=1,
    )
    always = jnp.ones((SUB_DEV,), bool)
    present = jnp.stack(
        [
            always,
            always & (row_pos > 0),
            always & (row_pos < row_count - 1),
            always & (col_pos > 0),
            always & (col_pos < col_count - 1),
            local > 0,
            local < SUB_DEV - 1,
        ],
        axis=1,
    )
    match = (
        neighbours[:, :, None] == jnp.arange(coarse_order.shape[0], dtype=jnp.int32)[None, None, :]
    )
    column_block = jnp.sum(jnp.where(match, coarse_order[None, None, :], 0), axis=-1)
    rows, select, share = panel_rows(blocks, column_block, present)
    assembled = lax.psum(share, ("row", "col"))
    panel = finish(rows, select, assembled)
    return (blocks.reshape(SUB_DEV, 7, NV * NV), panel)


def solution(mesh):
    in_specs = (
        P("row", "col", None, None),
        P("row", "col", None),
        P(),
        P("row", "col", None),
        P("row", "col", None),
        P("row", "col", None),
        P(),
    )
    out_specs = (P(("row", "col"), None, None), P(("row", "col"), None, None))
    return jax.shard_map(shards, mesh=mesh, in_specs=in_specs, out_specs=out_specs, check_vma=False)
```

profile of v0, /device:TPU:6, one launch (start us, length us, event | category | flops | bytes accessed | tf_op | source)
XLA Modules:
  0.0 590.4 jit_solution(2413078286542607056)
XLA Ops:
  7.2 2.8 fusion.121
  10.0 1.9 collective-permute-start
  11.9 3.6 collective-permute-start.1
  15.6 5.4 reshape.330
  21.0 2.6 fusion.118
  23.6 2.6 convert_subtract_fusion
  26.1 4.1 fusion.119
  30.8 5.3 reshape.326
  36.5 5.3 multiply_convert_fusion
  41.8 1.3 multiply_convert_fusion.1
  44.0 4.5 fusion.117
  52.7 1.5 copy.257
  55.7 1.3 multiply_convert_fusion.3
  57.8 4.5 convolution_bitcast_fusion.12
  62.3 1.6 convolution_bitcast_fusion.13
  63.9 1.2 copy.264
  65.5 2.2 copy.265
  70.2 1.8 slice_bitcast_fusion.1
  73.7 1.6 copy_convert_fusion
  76.0 1.2 fusion.24
  77.2 2.0 multiply_convert_fusion.2
  79.9 2.9 copy.249
  82.8 1.6 copy.253
  84.4 1.6 copy.245
  86.2 3.1 convolution_bitcast_fusion.1
  89.4 6.7 %reshape_squeeze.26 = bf16[8,16,4,4,4,48]{5,4,3,2,1,0:T(4,128)(2,1)} reshape(bf16[1,8,16,3072]{3,2,1,0:T(8,128)(2,1)} %collective-permute-done) | data formatting | bytes 1572864 | tf_op jit(solution)/shard_map/reshape;squeeze | solution.py:36
  96.1 1.3 slice.375
  100.9 6.2 %reshape_squeeze.27 = bf16[8,16,4,4,4,48]{5,4,3,2,1,0:T(4,128)(2,1)} reshape(bf16[1,8,16,3072]{3,2,1,0:T(8,128)(2,1)} %collective-permute-done.1) | data formatting | bytes 1572864 | tf_op jit(solution)/shard_map/reshape;squeeze | solution.py:36
  107.1 1.3 slice.376
  111.2 1.3 constant_dynamic-update-slice_fusion.2
  112.8 1.3 constant_dynamic-update-slice_fusion
  115.0 4.7 collective-permute-start.2
  119.7 1.5 collective-permute-start.3
  122.8 1.5 bitcast_dynamic-update-slice_fusion.7
  129.0 3.3 collective-permute-done.3
  134.6 1.3 bitcast_dynamic-update-slice_fusion.2
  135.9 1.3 bitcast_dynamic-update-slice_fusion.1
  140.9 1.6 copy.281
  145.4 259.5 %all-reduce.7.cloned.1.call-done = f32[528,528]{0,1:T(8,128)} async-done(((f32[528,528]{0,1:T(8,128)}), f32[528,528]{0,1:T(8,128)}) %all-reduce.7.cloned.1.call-update) | async-done | bytes 1115152 | tf_op jit(solution)/shard_map/psum | solution.py:207
  404.9 3.0 copy.282
  407.9 1.5 fusion.3
  411.2 11.9 %cholesky.134 = f32[128,128]{1,0:T(8,128)S(1)} custom-call(f32[128,128]{1,0:T(8,128)S(1)} %cholesky.346), custom_call_target="Cholesky" | custom-call | tf_op jit(solution)/shard_map/jit(cholesky)/cholesky | solution.py:131
  423.2 9.8 %custom-call.39 = f32[1,128,128]{1,2,0:T(8,128)S(1)} custom-call(f32[1,128,128]{2,1,0:T(8,128)S(1)} %get-tuple-element.54), custom_call_target="InvertDiagBlocksLowerTriangular" | custom-call | tf_op jit(solution)/shard_map/jit(cholesky)/cholesky | solution.py:131
  433.1 1.2 constant_dynamic-update-slice_fusion.18
  434.3 1.3 convolution_subtract_fusion
  435.6 11.7 %cholesky.274 = f32[128,128]{1,0:T(8,128)S(1)} custom-call(f32[128,128]{1,0:T(8,128)S(1)} %cholesky.350), custom_call_target="Cholesky" | custom-call | tf_op jit(solution)/shard_map/jit(cholesky)/cholesky | solution.py:131
  448.7 9.8 %custom-call.40 = f32[1,128,128]{1,2,0:T(8,128)S(1)} custom-call(f32[1,128,128]{2,1,0:T(8,128)S(1)} %get-tuple-element.51), custom_call_target="InvertDiagBlocksLowerTriangular" | custom-call | tf_op jit(solution)/shard_map/jit(cholesky)/cholesky | solution.py:131
  458.8 1.3 convolution_subtract_fusion.1
  460.1 12.1 %cholesky.295 = f32[128,128]{1,0:T(8,128)S(1)} custom-call(f32[128,128]{1,0:T(8,128)S(1)} %cholesky.355), custom_call_target="Cholesky" | custom-call | tf_op jit(solution)/shard_map/jit(cholesky)/cholesky | solution.py:131
  472.8 9.8 %custom-call.41 = f32[1,128,128]{1,2,0:T(8,128)S(1)} custom-call(f32[1,128,128]{2,1,0:T(8,128)S(1)} %get-tuple-element.48), custom_call_target="InvertDiagBlocksLowerTriangular" | custom-call | tf_op jit(solution)/shard_map/jit(cholesky)/cholesky | solution.py:131
  482.9 1.3 convolution_subtract_fusion.6
  484.1 11.7 %cholesky.314 = f32[128,128]{1,0:T(8,128)S(1)} custom-call(f32[128,128]{1,0:T(8,128)S(1)} %cholesky.360), custom_call_target="Cholesky" | custom-call | tf_op jit(solution)/shard_map/jit(cholesky)/cholesky | solution.py:131
  496.5 9.8 %custom-call.42 = f32[1,128,128]{1,2,0:T(8,128)S(1)} custom-call(f32[1,128,128]{2,1,0:T(8,128)S(1)} %get-tuple-element.45), custom_call_target="InvertDiagBlocksLowerTriangular" | custom-call | tf_op jit(solution)/shard_map/jit(cholesky)/cholesky | solution.py:131
  507.4 1.5 cholesky.334
  514.0 11.9 %while.1 = (s32[]{:T(128)}, f32[528,528]{1,0:T(8,128)}, s32[4,2]{0,1:T(2,128)S(1)}, f32[4,128,128]{2,1,0:T(8,128)S(1)}, s32[]{:T(128)}) while((s32[]{:T(128)}, f32[528,528]{1,0:T(8,128)}, s32[4,2]{0,1:T(2,128)S(1)}, f32[4,128,128]{2,1,0:T(8,128)S(1)}, s32[]{:T(128)}) %tuple.72), condition=%wide.while_cond, body=%wide.while_body.sunk | while | flops 2 | bytes 131181 | solution.py:133
  514.8 2.3 bitcast_dynamic-update-slice_fusion.9
  517.8 2.3 bitcast_dynamic-update-slice_fusion.9
  520.7 2.3 bitcast_dynamic-update-slice_fusion.9
  523.6 2.3 bitcast_dynamic-update-slice_fusion.9
  526.0 49.1 %custom-call.43 = f32[5,128,128]{1,2,0:T(8,128)S(1)} custom-call(f32[5,128,128]{2,1,0:T(8,128)S(1)} %pad_maximum_fusion), custom_call_target="InvertDiagBlocksLowerTriangular" | custom-call | tf_op jit(solution)/shard_map/jit(_solve_triangular)/triangular_solve | solution.py:133
  576.8 1.2 convolution_subtract_fusion.5
  578.3 1.3 convolution_subtract_fusion.4
  579.9 1.2 convolution_subtract_fusion.3
  581.3 1.2 fusion.5
  (268 shorter events, 50.6 us)
Async XLA Ops:
  7.2 8.4 %copy-start.3 = (bf16[2,8,16,3072]{3,2,1,0:T(8,128)(2,1)S(1)}, bf16[2,8,16,3072]{3,2,1,0:T(8,128)(2,1)}, u32[]{:S(2)}) copy-start(bf16[2,8,16,3072]{3,2,1,0:T(8,128)(2,1)} %param.8) | copy-start | bytes 4718596
  7.2 397.8 %all-reduce.7.cloned.1.call-start = ((), (), s32[]{:S(2)}) async-start(), calls=%async_computation | async-start | bytes 2703360 | tf_op jit(solution)/shard_map/psum | solution.py:207
  10.0 79.4 %collective-permute-start = (bf16[1,8,16,3072]{3,2,1,0:T(8,128)(2,1)}, bf16[1,8,16,3072]{3,2,1,0:T(8,128)(2,1)}, u32[]{:S(2)}, u32[]{:S(2)}) collective-permute-start(bf16[1,8,16,3072]{3,2,1,0:T(8,128)(2,1)} %get-tuple-element.43), channel_id=1, source_target_pairs={{0,32},{32,64},{64,96},{96,128},{128,160},{160,192},{192,224},{1,3... | collective-permute-start | bytes 2359304 | tf_op jit(solution)/shard_map/ppermute | solution.py:19
  11.9 88.9 %collective-permute-start.1 = (bf16[1,8,16,3072]{3,2,1,0:T(8,128)(2,1)}, bf16[1,8,16,3072]{3,2,1,0:T(8,128)(2,1)}, u32[]{:S(2)}, u32[]{:S(2)}) collective-permute-start(bf16[1,8,16,3072]{3,2,1,0:T(8,128)(2,1)} %get-tuple-element.42), channel_id=1, source_target_pairs={{32,0},{64,32},{96,64},{128,96},{160,128},{192,160},{224,192},{33,... | collective-permute-start | bytes 2359304 | tf_op jit(solution)/shard_map/ppermute | solution.py:20
  26.1 4.1 copy-start.40
  30.3 5.8 copy-start.36
  30.8 5.3 copy-start.45
  30.8 5.5 copy-start.41
  30.8 5.7 copy-start.35
  36.5 5.3 copy-start
  41.8 2.2 copy-start.2
  44.0 8.1 %copy-start.39 = (f32[3,8,16]{2,1,0:T(8,128)S(1)}, f32[3,8,16]{2,1,0:T(8,128)}, u32[]{:S(2)}) copy-start(f32[3,8,16]{2,1,0:T(8,128)} %param.11) | copy-start | bytes 4612
  52.1 2.1 copy-start.12
  62.3 1.6 copy-start.6
  63.9 1.6 copy-start.5
  65.1 4.1 copy-start.19
  65.5 2.2 copy-start.42
  67.7 4.3 copy-start.54
  67.7 4.3 copy-start.55
  67.7 4.3 copy-start.56
  67.7 4.3 copy-start.57
  67.7 4.3 copy-start.58
  67.7 4.3 copy-start.59
  67.7 4.3 copy-start.60
  67.7 4.3 copy-start.46
  67.7 4.7 copy-start.34
  67.7 6.0 %copy-start.17 = (bf16[1,8,16,1,4,4,48]{6,5,4,3,2,1,0:T(4,128)(2,1)S(1)}, bf16[1,8,16,1,4,4,48]{6,5,4,3,2,1,0:T(4,128)(2,1)}, u32[]{:S(2)}) copy-start(bf16[1,8,16,1,4,4,48]{6,5,4,3,2,1,0:T(4,128)(2,1)} %get-tuple-element.36) | copy-start | bytes 589828
  67.8 6.0 %copy-start.18 = (bf16[1,8,16,1,4,4,48]{6,5,4,3,2,1,0:T(4,128)(2,1)S(1)}, bf16[1,8,16,1,4,4,48]{6,5,4,3,2,1,0:T(4,128)(2,1)}, u32[]{:S(2)}) copy-start(bf16[1,8,16,1,4,4,48]{6,5,4,3,2,1,0:T(4,128)(2,1)} %get-tuple-element.37) | copy-start | bytes 589828
  67.9 2.3 copy-start.32
  68.5 1.7 copy-start.47
  70.2 5.5 copy-start.15
  70.2 5.8 copy-start.21
  72.4 3.0 copy-start.38
  72.4 3.0 copy-start.50
  73.7 3.4 copy-start.1
  79.9 2.9 copy-start.8
  82.8 1.6 copy-start.9
  84.4 1.6 slice-start.2
  84.4 1.7 copy-start.52
  84.4 1.7 copy-start.53
  96.1 2.0 copy-start.11
  96.1 2.0 copy-start.37
  107.1 2.0 copy-start.10
  110.9 1.7 copy-start.4
  112.8 8.4 %copy-start.20 = (f32[1,8,16,1,4,4,48]{6,1,5,4,2,3,0:T(8,128)S(1)}, f32[1,8,16,1,4,4,48]{6,1,5,4,2,3,0:T(8,128)}, u32[]{:S(2)}) copy-start(f32[1,8,16,1,4,4,48]{6,1,5,4,2,3,0:T(8,128)} %copy.245) | copy-start | bytes 1179652
  112.8 8.4 %copy-start.43 = (f32[1,8,16]{1,2,0:T(8,128)S(1)}, f32[1,8,16]{1,2,0:T(8,128)}, u32[]{:S(2)}) copy-start(f32[1,8,16]{1,2,0:T(8,128)} %get-tuple-element.55) | copy-start | bytes 1540
  112.8 8.4 %copy-start.64 = (f32[4,48,48]{2,1,0:T(8,128)S(1)}, f32[4,48,48]{2,1,0:T(8,128)}, u32[]{:S(2)}) copy-start(f32[4,48,48]{2,1,0:T(8,128)} %convolution_bitcast_fusion.10) | copy-start | bytes 110596
  115.0 6.7 %copy-start.28 = (f32[4,48,48]{2,1,0:T(8,128)S(1)}, f32[4,48,48]{2,1,0:T(8,128)}, u32[]{:S(2)}) copy-start(f32[4,48,48]{2,1,0:T(8,128)} %convolution_bitcast_fusion.12) | copy-start | bytes 110596
  115.0 6.7 %copy-start.29 = (f32[4,48,48]{2,1,0:T(8,128)S(1)}, f32[4,48,48]{2,1,0:T(8,128)}, u32[]{:S(2)}) copy-start(f32[4,48,48]{2,1,0:T(8,128)} %convolution_bitcast_fusion.13) | copy-start | bytes 110596
  115.0 6.7 %copy-start.33 = (f32[4,48,48]{2,1,0:T(8,128)S(1)}, f32[4,48,48]{2,1,0:T(8,128)}, u32[]{:S(2)}) copy-start(f32[4,48,48]{2,1,0:T(8,128)} %fusion.24) | copy-start | bytes 110596
  115.0 12.5 %collective-permute-start.2 = (bf16[4,1,16,3072]{3,2,1,0:T(8,128)(2,1)}, bf16[4,1,16,3072]{3,2,1,0:T(8,128)(2,1)}, u32[]{:S(2)}, u32[]{:S(2)}) collective-permute-start(bf16[4,1,16,3072]{3,2,1,0:T(8,128)(2,1)} %get-tuple-element.41), channel_id=1, source_target_pairs={{0,1},{1,2},{2,3},{3,4},{4,5},{5,6},{6,7},{7,8},{8,9},{9,10},{10,1... | collective-permute-start | bytes 1179656 | tf_op jit(solution)/shard_map/ppermute | solution.py:19
  119.7 12.6 %collective-permute-start.3 = (bf16[4,1,16,3072]{3,2,1,0:T(8,128)(2,1)}, bf16[4,1,16,3072]{3,2,1,0:T(8,128)(2,1)}, u32[]{:S(2)}, u32[]{:S(2)}) collective-permute-start(bf16[4,1,16,3072]{3,2,1,0:T(8,128)(2,1)} %get-tuple-element.40), channel_id=1, source_target_pairs={{1,0},{2,1},{3,2},{4,3},{5,4},{6,5},{7,6},{8,7},{9,8},{10,9},{11,1... | collective-permute-start | bytes 1179656 | tf_op jit(solution)/shard_map/ppermute | solution.py:20
  122.8 1.5 copy-start.25
  122.8 1.5 copy-start.27
  124.3 1.2 copy-start.24
  125.8 8.1 %copy-start.16 = (f32[1,2,16,16,48]{4,2,3,0,1:T(8,128)S(1)}, f32[1,2,16,16,48]{4,2,3,0,1:T(8,128)}, u32[]{:S(2)}) copy-start(f32[1,2,16,16,48]{4,2,3,0,1:T(8,128)} %slice_convert_fusion.1) | copy-start | bytes 294916
  129.0 5.6 slice-start
  133.8 2.0 slice-start.1
  133.9 2.0 copy-start.48
  404.9 3.0 copy-start.7
  410.1 1.1 copy-start.14
  512.7 1.3 copy-start.30
  512.7 13.2 %copy-start.31 = (f32[128,112]{1,0:T(8,128)S(1)}, f32[128,112]{1,0:T(8,128)}, u32[]{:S(2)}) copy-start(f32[128,112]{1,0:T(8,128)} %pad_convert_fusion) | copy-start | bytes 172036
  576.5 4.8 copy-start.61
  (10 other events, 9.2 us)
Sparse Core Ops, SparseCore 0:
  142.6 262.2 all-reduce.6
where the time goes:
time: 597 us; the launch traced here: 590 us
  waiting for transfers between devices  264 us (44%)
  other arithmetic  157 us (26%)
  local copies, waits for them, and re-layouts  95.1 us (16%)
  matrix products  44.6 us (7%)
  between operations  18.6 us (3%)
  starting transfers between devices  11.8 us (2%)
    psum x1, waiting for transfers between devices, shards(): assembled = lax.psum(share, ('row', 'col'))  259 us
    another operation x19, other arithmetic, finish(): factor = jnp.linalg.cholesky(0.5 * (whole + whole.T))  91.6 us
    another operation x7, other arithmetic, finish(): jax.scipy.linalg.solve_triangular(factor, rows.reshape(count * NV, PB * N...  50.7 us
    dot_general x21, matrix products, contract(): return jnp.einsum(form, left, right, preferred_element_type=jnp.float32)  28.5 us
    slice x10, local copies, waits for them, and re-layouts, traces(): picked = lax.index_in_dim(nodes, side, lead + axis, keepdims=False)  16.6 us
    another operation x4, local copies, waits for them, and re-layouts, traces(): nodes = values.reshape(values.shape[:lead] + (4, 4, 4, NV))  14 us
    unnamed x143, local copies, waits for them, and re-layouts  12.1 us
  transfers between devices with their start and end apart: 5, of which 3 were waited for; matrix products, arithmetic and copies ran while one was open for 15% of the time, Pallas kernels for 0%

commit v1 on v0

--- a/solution.py
+++ b/solution.py
@@ -204,7 +204,7 @@
     )
     column_block = jnp.sum(jnp.where(match, coarse_order[None, None, :], 0), axis=-1)
     rows, select, share = panel_rows(blocks, column_block, present)
-    assembled = lax.psum(share, ("row", "col"))
+    assembled = lax.psum(lax.psum(share, "col"), "row")
     panel = finish(rows, select, assembled)
     return (blocks.reshape(SUB_DEV, 7, NV * NV), panel)
 

time: 597 us -> 557 us (0.933)
  waiting for transfers between devices: 264 us -> 222 us
    psum x1 -> x2, waiting for transfers between devices: 259 us -> 216 us  [shards(): assembled = lax.psum(lax.psum(share, 'col'), 'row')]
    unnamed x143 -> x141, local copies, waits for them, and re-layouts: 12.1 us -> 10.4 us
  transfers between devices with their start and end apart: 5 -> 6, of which waited for: 3 -> 4; matrix products, arithmetic and copies ran while one was open for 15% -> 16% of each run, Pallas kernels for 0% -> 0%
where the time goes in v1:
time: 557 us; the launch traced here: 547 us
  waiting for transfers between devices  222 us (40%)
  other arithmetic  156 us (28%)
  local copies, waits for them, and re-layouts  93.3 us (17%)
  matrix products  45.4 us (8%)
  between operations  19 us (3%)
  starting transfers between devices  11.8 us (2%)
    psum x2, waiting for transfers between devices, shards(): assembled = lax.psum(lax.psum(share, 'col'), 'row')  216 us
    another operation x19, other arithmetic, finish(): factor = jnp.linalg.cholesky(0.5 * (whole + whole.T))  91.6 us
    another operation x7, other arithmetic, finish(): jax.scipy.linalg.solve_triangular(factor, rows.reshape(count * NV, PB * N...  51.2 us
    dot_general x21, matrix products, contract(): return jnp.einsum(form, left, right, preferred_element_type=jnp.float32)  27.9 us
    slice x10, local copies, waits for them, and re-layouts, traces(): picked = lax.index_in_dim(nodes, side, lead + axis, keepdims=False)  16.5 us
    another operation x4, local copies, waits for them, and re-layouts, traces(): nodes = values.reshape(values.shape[:lead] + (4, 4, 4, NV))  13.9 us
    another operation x13, local copies, waits for them, and re-layouts  12 us
  transfers between devices with their start and end apart: 6, of which 4 were waited for; matrix products, arithmetic and copies ran while one was open for 16% of the time, Pallas kernels for 0%

profile of v1, /device:TPU:6, one launch (start us, length us, event | category | flops | bytes accessed | tf_op | source)
XLA Modules:
  0.0 547.3 jit_solution(5035964121212085930)
XLA Ops:
  7.2 2.8 fusion.121
  10.0 1.9 collective-permute-start
  11.9 3.6 collective-permute-start.1
  15.6 5.4 reshape.330
  21.0 2.6 fusion.118
  23.6 2.6 convert_subtract_fusion
  26.1 4.1 fusion.119
  30.3 5.3 reshape.326
  36.0 5.3 multiply_convert_fusion
  41.3 1.3 multiply_convert_fusion.1
  43.5 4.5 fusion.117
  52.1 1.5 copy.257
  55.0 1.3 multiply_convert_fusion.3
  56.5 4.4 convolution_bitcast_fusion.12
  61.0 1.6 convolution_bitcast_fusion.13
  64.2 2.2 copy.265
  68.9 1.8 slice_bitcast_fusion.1
  72.4 1.6 copy_convert_fusion
  75.8 2.0 multiply_convert_fusion.2
  78.4 2.9 copy.249
  81.3 1.6 copy.253
  82.9 1.6 copy.245
  85.3 3.3 convolution_bitcast_fusion.1
  88.6 6.6 %reshape_squeeze.26 = bf16[8,16,4,4,4,48]{5,4,3,2,1,0:T(4,128)(2,1)} reshape(bf16[1,8,16,3072]{3,2,1,0:T(8,128)(2,1)} %collective-permute-done) | data formatting | bytes 1572864 | tf_op jit(solution)/shard_map/reshape;squeeze | solution.py:36
  95.2 1.3 slice.375
  99.4 6.2 %reshape_squeeze.27 = bf16[8,16,4,4,4,48]{5,4,3,2,1,0:T(4,128)(2,1)} reshape(bf16[1,8,16,3072]{3,2,1,0:T(8,128)(2,1)} %collective-permute-done.1) | data formatting | bytes 1572864 | tf_op jit(solution)/shard_map/reshape;squeeze | solution.py:36
  105.6 1.3 slice.376
  108.2 1.3 constant_dynamic-update-slice_fusion.2
  109.7 1.3 constant_dynamic-update-slice_fusion
  112.0 4.7 collective-permute-start.2
  116.7 1.3 collective-permute-start.3
  119.6 1.5 bitcast_dynamic-update-slice_fusion.7
  122.6 1.9 collective-permute-done.2
  126.0 3.3 collective-permute-done.3
  131.5 1.3 bitcast_dynamic-update-slice_fusion.2
  132.9 1.3 bitcast_dynamic-update-slice_fusion.1
  135.9 2.4 fusion.33
  140.4 153.3 %all-reduce.8.cloned.1.call-done = f32[11,48,528]{2,0,1:T(8,128)} async-done(((f32[11,48,528]{2,0,1:T(8,128)}), f32[11,48,528]{2,0,1:T(8,128)}) %all-reduce.8.cloned.1.call-update) | async-done | bytes 1115152 | tf_op jit(solution)/shard_map/psum | solution.py:207
  293.8 2.0 copy.280
  295.8 1.6 copy.281
  298.1 63.1 %all-reduce.10.cloned.1.call-done = f32[528,528]{0,1:T(8,128)} async-done(((f32[528,528]{0,1:T(8,128)}), f32[528,528]{0,1:T(8,128)}) %all-reduce.10.cloned.1.call-update) | async-done | bytes 1115152 | tf_op jit(solution)/shard_map/psum | solution.py:207
  361.2 3.0 copy.282
  364.2 1.5 fusion.3
  367.5 11.7 %cholesky.134 = f32[128,128]{1,0:T(8,128)S(1)} custom-call(f32[128,128]{1,0:T(8,128)S(1)} %cholesky.346), custom_call_target="Cholesky" | custom-call | tf_op jit(solution)/shard_map/jit(cholesky)/cholesky | solution.py:131
  379.3 9.8 %custom-call.39 = f32[1,128,128]{1,2,0:T(8,128)S(1)} custom-call(f32[1,128,128]{2,1,0:T(8,128)S(1)} %get-tuple-element.54), custom_call_target="InvertDiagBlocksLowerTriangular" | custom-call | tf_op jit(solution)/shard_map/jit(cholesky)/cholesky | solution.py:131
  389.2 1.2 constant_dynamic-update-slice_fusion.18
  390.4 1.3 convolution_subtract_fusion
  391.7 11.9 %cholesky.274 = f32[128,128]{1,0:T(8,128)S(1)} custom-call(f32[128,128]{1,0:T(8,128)S(1)} %cholesky.350), custom_call_target="Cholesky" | custom-call | tf_op jit(solution)/shard_map/jit(cholesky)/cholesky | solution.py:131
  405.0 9.8 %custom-call.40 = f32[1,128,128]{1,2,0:T(8,128)S(1)} custom-call(f32[1,128,128]{2,1,0:T(8,128)S(1)} %get-tuple-element.51), custom_call_target="InvertDiagBlocksLowerTriangular" | custom-call | tf_op jit(solution)/shard_map/jit(cholesky)/cholesky | solution.py:131
  415.1 1.3 convolution_subtract_fusion.1
  416.4 11.7 %cholesky.295 = f32[128,128]{1,0:T(8,128)S(1)} custom-call(f32[128,128]{1,0:T(8,128)S(1)} %cholesky.355), custom_call_target="Cholesky" | custom-call | tf_op jit(solution)/shard_map/jit(cholesky)/cholesky | solution.py:131
  428.8 9.8 %custom-call.41 = f32[1,128,128]{1,2,0:T(8,128)S(1)} custom-call(f32[1,128,128]{2,1,0:T(8,128)S(1)} %get-tuple-element.48), custom_call_target="InvertDiagBlocksLowerTriangular" | custom-call | tf_op jit(solution)/shard_map/jit(cholesky)/cholesky | solution.py:131
  438.9 1.3 convolution_subtract_fusion.6
  440.2 11.9 %cholesky.314 = f32[128,128]{1,0:T(8,128)S(1)} custom-call(f32[128,128]{1,0:T(8,128)S(1)} %cholesky.360), custom_call_target="Cholesky" | custom-call | tf_op jit(solution)/shard_map/jit(cholesky)/cholesky | solution.py:131
  452.8 9.8 %custom-call.42 = f32[1,128,128]{1,2,0:T(8,128)S(1)} custom-call(f32[1,128,128]{2,1,0:T(8,128)S(1)} %get-tuple-element.45), custom_call_target="InvertDiagBlocksLowerTriangular" | custom-call | tf_op jit(solution)/shard_map/jit(cholesky)/cholesky | solution.py:131
  463.6 1.5 cholesky.334
  470.4 12.1 %while.1 = (s32[]{:T(128)}, f32[528,528]{1,0:T(8,128)}, s32[4,2]{0,1:T(2,128)S(1)}, f32[4,128,128]{2,1,0:T(8,128)S(1)}, s32[]{:T(128)}) while((s32[]{:T(128)}, f32[528,528]{1,0:T(8,128)}, s32[4,2]{0,1:T(2,128)S(1)}, f32[4,128,128]{2,1,0:T(8,128)S(1)}, s32[]{:T(128)}) %tuple.74), condition=%wide.while_cond, body=%wide.while_body.sunk | while | flops 2 | bytes 131181 | solution.py:133
  471.1 2.3 bitcast_dynamic-update-slice_fusion.9
  474.1 2.3 bitcast_dynamic-update-slice_fusion.9
  477.2 2.3 bitcast_dynamic-update-slice_fusion.9
  480.2 2.3 bitcast_dynamic-update-slice_fusion.9
  482.7 49.1 %custom-call.43 = f32[5,128,128]{1,2,0:T(8,128)S(1)} custom-call(f32[5,128,128]{2,1,0:T(8,128)S(1)} %pad_maximum_fusion), custom_call_target="InvertDiagBlocksLowerTriangular" | custom-call | tf_op jit(solution)/shard_map/jit(_solve_triangular)/triangular_solve | solution.py:133
  533.4 1.2 convolution_subtract_fusion.5
  534.9 1.4 convolution_subtract_fusion.4
  (269 shorter events, 48.8 us)
Async XLA Ops:
  7.2 8.4 %copy-start.3 = (bf16[2,8,16,3072]{3,2,1,0:T(8,128)(2,1)S(1)}, bf16[2,8,16,3072]{3,2,1,0:T(8,128)(2,1)}, u32[]{:S(2)}) copy-start(bf16[2,8,16,3072]{3,2,1,0:T(8,128)(2,1)} %param.8) | copy-start | bytes 4718596
  7.2 286.6 %all-reduce.8.cloned.1.call-start = ((), (), s32[]{:S(2)}) async-start(), calls=%async_computation | async-start | bytes 3932160 | tf_op jit(solution)/shard_map/psum | solution.py:207
  10.0 78.6 %collective-permute-start = (bf16[1,8,16,3072]{3,2,1,0:T(8,128)(2,1)}, bf16[1,8,16,3072]{3,2,1,0:T(8,128)(2,1)}, u32[]{:S(2)}, u32[]{:S(2)}) collective-permute-start(bf16[1,8,16,3072]{3,2,1,0:T(8,128)(2,1)} %get-tuple-element.43), channel_id=1, source_target_pairs={{0,32},{32,64},{64,96},{96,128},{128,160},{160,192},{192,224},{1,3... | collective-permute-start | bytes 2359304 | tf_op jit(solution)/shard_map/ppermute | solution.py:19
  11.9 87.4 %collective-permute-start.1 = (bf16[1,8,16,3072]{3,2,1,0:T(8,128)(2,1)}, bf16[1,8,16,3072]{3,2,1,0:T(8,128)(2,1)}, u32[]{:S(2)}, u32[]{:S(2)}) collective-permute-start(bf16[1,8,16,3072]{3,2,1,0:T(8,128)(2,1)} %get-tuple-element.42), channel_id=1, source_target_pairs={{32,0},{64,32},{96,64},{128,96},{160,128},{192,160},{224,192},{33,... | collective-permute-start | bytes 2359304 | tf_op jit(solution)/shard_map/ppermute | solution.py:20
  26.1 4.1 copy-start.37
  30.3 5.4 copy-start.33
  30.3 5.3 copy-start.43
  30.3 5.6 %copy-start.38 = (f32[2,8,16]{2,1,0:T(8,128)S(1)}, f32[2,8,16]{2,1,0:T(8,128)}, u32[]{:S(2)}) copy-start(f32[2,8,16]{2,1,0:T(8,128)} %param.9) | copy-start | bytes 3076
  30.3 5.7 %copy-start.32 = (bf16[3,64,64]{2,1,0:T(8,128)(2,1)S(1)}, bf16[3,64,64]{2,1,0:T(8,128)(2,1)}, u32[]{:S(2)}) copy-start(bf16[3,64,64]{2,1,0:T(8,128)(2,1)} %param.10) | copy-start | bytes 73732
  36.0 5.3 copy-start
  41.3 2.2 copy-start.2
  43.5 7.9 %copy-start.36 = (f32[3,8,16]{2,1,0:T(8,128)S(1)}, f32[3,8,16]{2,1,0:T(8,128)}, u32[]{:S(2)}) copy-start(f32[3,8,16]{2,1,0:T(8,128)} %param.11) | copy-start | bytes 4612
  51.5 2.2 copy-start.12
  61.0 1.6 copy-start.6
  62.6 1.6 copy-start.5
  63.8 4.1 copy-start.19
  64.2 2.2 copy-start.39
  66.4 4.3 copy-start.54
  66.4 4.3 copy-start.55
  66.4 4.3 copy-start.56
  66.4 4.3 copy-start.57
  66.4 4.3 copy-start.58
  66.4 4.3 copy-start.59
  66.4 4.3 copy-start.44
  66.4 4.6 copy-start.31
  66.4 5.9 %copy-start.17 = (bf16[1,8,16,1,4,4,48]{6,5,4,3,2,1,0:T(4,128)(2,1)S(1)}, bf16[1,8,16,1,4,4,48]{6,5,4,3,2,1,0:T(4,128)(2,1)}, u32[]{:S(2)}) copy-start(bf16[1,8,16,1,4,4,48]{6,5,4,3,2,1,0:T(4,128)(2,1)} %get-tuple-element.36) | copy-start | bytes 589828
  66.5 5.9 %copy-start.18 = (bf16[1,8,16,1,4,4,48]{6,5,4,3,2,1,0:T(4,128)(2,1)S(1)}, bf16[1,8,16,1,4,4,48]{6,5,4,3,2,1,0:T(4,128)(2,1)}, u32[]{:S(2)}) copy-start(bf16[1,8,16,1,4,4,48]{6,5,4,3,2,1,0:T(4,128)(2,1)} %get-tuple-element.37) | copy-start | bytes 589828
  66.6 2.3 copy-start.29
  67.2 3.5 copy-start.45
  68.9 5.4 copy-start.15
  68.9 5.7 %copy-start.21 = (bf16[7,2,16,16,48]{4,2,3,0,1:T(8,128)(2,1)S(1)}, bf16[7,2,16,16,48]{4,2,3,0,1:T(8,128)(2,1)}, u32[]{:S(2)}) copy-start(bf16[7,2,16,16,48]{4,2,3,0,1:T(8,128)(2,1)} %multiply_convert_fusion.3) | copy-start | bytes 1032196
  71.1 2.9 copy-start.50
  72.4 3.4 copy-start.1
  78.4 2.9 copy-start.8
  81.3 1.6 copy-start.9
  82.9 1.6 slice-start.2
  82.9 1.7 copy-start.52
  82.9 1.7 copy-start.53
  95.2 2.0 copy-start.11
  95.2 2.0 copy-start.35
  105.6 2.0 copy-start.10
  105.6 2.0 copy-start.34
  107.9 1.7 copy-start.4
  109.7 8.3 %copy-start.20 = (f32[1,8,16,1,4,4,48]{6,1,5,4,2,3,0:T(8,128)S(1)}, f32[1,8,16,1,4,4,48]{6,1,5,4,2,3,0:T(8,128)}, u32[]{:S(2)}) copy-start(f32[1,8,16,1,4,4,48]{6,1,5,4,2,3,0:T(8,128)} %copy.245) | copy-start | bytes 1179652
  109.7 8.3 %copy-start.40 = (f32[1,8,16]{1,2,0:T(8,128)S(1)}, f32[1,8,16]{1,2,0:T(8,128)}, u32[]{:S(2)}) copy-start(f32[1,8,16]{1,2,0:T(8,128)} %get-tuple-element.55) | copy-start | bytes 1540
  112.0 6.5 %copy-start.25 = (f32[4,48,48]{2,1,0:T(8,128)S(1)}, f32[4,48,48]{2,1,0:T(8,128)}, u32[]{:S(2)}) copy-start(f32[4,48,48]{2,1,0:T(8,128)} %convolution_bitcast_fusion.12) | copy-start | bytes 110596
  112.0 6.5 %copy-start.26 = (f32[4,48,48]{2,1,0:T(8,128)S(1)}, f32[4,48,48]{2,1,0:T(8,128)}, u32[]{:S(2)}) copy-start(f32[4,48,48]{2,1,0:T(8,128)} %convolution_bitcast_fusion.13) | copy-start | bytes 110596
  112.0 6.5 %copy-start.30 = (f32[4,48,48]{2,1,0:T(8,128)S(1)}, f32[4,48,48]{2,1,0:T(8,128)}, u32[]{:S(2)}) copy-start(f32[4,48,48]{2,1,0:T(8,128)} %fusion.24) | copy-start | bytes 110596
  112.0 12.5 %collective-permute-start.2 = (bf16[4,1,16,3072]{3,2,1,0:T(8,128)(2,1)}, bf16[4,1,16,3072]{3,2,1,0:T(8,128)(2,1)}, u32[]{:S(2)}, u32[]{:S(2)}) collective-permute-start(bf16[4,1,16,3072]{3,2,1,0:T(8,128)(2,1)} %get-tuple-element.41), channel_id=1, source_target_pairs={{0,1},{1,2},{2,3},{3,4},{4,5},{5,6},{6,7},{7,8},{8,9},{9,10},{10,1... | collective-permute-start | bytes 1179656 | tf_op jit(solution)/shard_map/ppermute | solution.py:19
  116.7 12.6 %collective-permute-start.3 = (bf16[4,1,16,3072]{3,2,1,0:T(8,128)(2,1)}, bf16[4,1,16,3072]{3,2,1,0:T(8,128)(2,1)}, u32[]{:S(2)}, u32[]{:S(2)}) collective-permute-start(bf16[4,1,16,3072]{3,2,1,0:T(8,128)(2,1)} %get-tuple-element.40), channel_id=1, source_target_pairs={{1,0},{2,1},{3,2},{4,3},{5,4},{6,5},{7,6},{8,7},{9,8},{10,9},{11,1... | collective-permute-start | bytes 1179656 | tf_op jit(solution)/shard_map/ppermute | solution.py:20
  119.5 1.5 copy-start.22
  119.6 1.5 copy-start.24
  121.7 9.2 %copy-start.16 = (f32[1,2,16,16,48]{4,2,3,0,1:T(8,128)S(1)}, f32[1,2,16,16,48]{4,2,3,0,1:T(8,128)}, u32[]{:S(2)}) copy-start(f32[1,2,16,16,48]{4,2,3,0,1:T(8,128)} %slice_convert_fusion.1) | copy-start | bytes 294916
  125.9 5.6 %slice-start = ((bf16[2,8,4,16,48]{4,1,3,2,0:T(8,128)(2,1)}), bf16[2,8,3,16,48]{4,1,3,2,0:T(8,128)(2,1)S(1)}, s32[]{:S(2)}) async-start(bf16[2,8,4,16,48]{4,1,3,2,0:T(8,128)(2,1)} %slice_bitcast_fusion), calls=%async_computation.2 | async-start | bytes 393216 | tf_op jit(solution)/shard_map/slice | solution.py:87
  126.0 5.6 %copy-start.48 = (f32[2,8,4]{1,2,0:T(4,128)S(1)}, f32[2,8,4]{1,2,0:T(4,128)}, u32[]{:S(2)}) copy-start(f32[2,8,4]{1,2,0:T(4,128)} %get-tuple-element.66) | copy-start | bytes 772
  130.8 2.0 slice-start.1
  130.8 2.0 copy-start.46
  131.5 2.6 copy-start.49
  138.4 222.8 %all-reduce.10.cloned.1.call-start = ((), (), s32[]{:S(2)}) async-start(), calls=%async_computation.1 | async-start | bytes 2703360 | tf_op jit(solution)/shard_map/psum | solution.py:207
  361.2 3.0 copy-start.7
  366.4 1.1 copy-start.14
  469.1 1.3 copy-start.27
  469.1 13.4 %copy-start.28 = (f32[128,112]{1,0:T(8,128)S(1)}, f32[128,112]{1,0:T(8,128)}, u32[]{:S(2)}) copy-start(f32[128,112]{1,0:T(8,128)} %pad_convert_fusion) | copy-start | bytes 172036
  533.2 4.8 copy-start.60
  (10 other events, 8.6 us)
Sparse Core Ops, SparseCore 0:
  138.5 155.2 all-reduce.7
  297.5 63.7 all-reduce.9
